TPU v7x, 32 devices: a whole 2x2x4 slice. The times are simulated.
32 devices in a mesh: grp: 2 (over x), space: 16 (over z, y, core).
Axes of the slice: x: 2, y: 2, z: 4, core: 2. Of those that a mesh axis runs over, the one named last changes fastest.
Arguments:
- vectors: bfloat16 [4, 128, 6, 16, 256], P('grp', None, None, 'space'), parts along dimension 0, may hold values from -6 to 6
- gauge_links: float32 [3, 18, 4, 16, 256], P(None, None, 'grp', 'space'), parts along dimension 2, may hold values from -1.5 to 2.5, as said below
- perambulators: bfloat16 [4, 2, 2, 128, 128], P('grp'), parts along dimension 0, may hold values from -0.046875 to 0.046875
- time_pairs: int32 [16, 2], P('grp'), parts along dimension 0, may hold values from 0 to 1
- ordering: int32 [4, 128], P('grp'), parts along dimension 0, may hold values from 0 to 127, each once within a row
- op_momenta: int32 [4, 3], replicated, may hold values from -2 to 2
Outputs:
- elementals: float32 [8, 512, 128], P('grp', 'space'), parts along dimension 0
- correlators: float32 [8, 8, 2], P('grp'), parts along dimension 0
There are 2 independent parts, one for each index of `grp`. A program takes and returns all parts, laid end to end along the dimension named above; an argument that names none is the same for every part. Nothing has to cross between parts.
Inputs may be any that keep to these rules, and one draw needn't show every extreme that they name: `gauge_links`: components ordered as row, column, then real or imaginary part of 3 x 3 complex matrices.
All inputs are finite; a program needn't handle non-finite values.
Results may differ from a plain program's by a relative error of at most 0.0051.
Values may be sent and summed in bfloat16 or wider, within the bound.
No kernel may reach another device: no remote copies, remote signals or barrier semaphores. Data moves between devices by JAX's collectives and lax.ppermute only.
A program may use at most 128 MiB of HBM per device.

v0:
```python
import math

import jax
import jax.numpy as jnp
from jax import lax
from jax.experimental import pallas as pl
from jax.experimental.pallas import tpu as pltpu
from jax.sharding import PartitionSpec as P


LY = 16
LZ = 16
RHO = 0.1


F32 = jnp.float32
BF16 = jnp.bfloat16


def vmem():
    return pl.BlockSpec(memory_space=pltpu.VMEM)


def smem():
    return pl.BlockSpec(memory_space=pltpu.SMEM)


def call(kernel, outs, ins, scalars=0, scratch=(), loose=0, flops=1000000, limit=16 << 20):
    run = pl.pallas_call(
        kernel,
        out_shape=[jax.ShapeDtypeStruct(s, d) for s, d in outs],
        in_specs=[smem()] * scalars
        + [vmem()] * (len(ins) - scalars - loose)
        + [pl.BlockSpec(memory_space=pltpu.HBM)] * loose,
        out_specs=[vmem()] * len(outs),
        scratch_shapes=list(scratch),
        compiler_params=pltpu.CompilerParams(vmem_limit_bytes=limit),
        cost_estimate=pl.CostEstimate(flops=flops, bytes_accessed=1000000, transcendentals=0),
    )
    first = len(ins) - loose
    ins = ins[:first] + [pltpu.with_memory_space_constraint(x, pltpu.HBM) for x in ins[first:]]
    return run(*ins)


def shifted(value, by):
    size = lax.axis_size("space")
    return lax.ppermute(value, "space", [(i, (i + by) % size) for i in range(size)])


def swapped(value, bit):
    size = lax.axis_size("space")
    return lax.ppermute(value, "space", [(i, i ^ bit) for i in range(size)])


def cmul(x, y):
    return (x[0] * y[0] - x[1] * y[1], x[0] * y[1] + x[1] * y[0])


def cadd(x, y):
    return (x[0] + y[0], x[1] + y[1])


def conj_mul(x, y):
    return (x[0] * y[0] + x[1] * y[1], x[0] * y[1] - x[1] * y[0])


def mul_conj(x, y):
    return (x[0] * y[0] + x[1] * y[1], x[1] * y[0] - x[0] * y[1])


def total(terms):
    out = terms[0]
    for t in terms[1:]:
        out = cadd(out, t)
    return out


R3 = range(3)


def mm(x, y):
    return [[total([cmul(x[a][c], y[c][b]) for c in R3]) for b in R3] for a in R3]


def mm_h(x, y):
    return [[total([mul_conj(x[a][c], y[b][c]) for c in R3]) for b in R3] for a in R3]


def h_mm(x, y):
    return [[total([conj_mul(x[c][a], y[c][b]) for c in R3]) for b in R3] for a in R3]


OFF = ((0, 1), (0, 2), (1, 2))


def anti(entry, imag):
    out = [imag(a, a) for a in R3]
    for a, b in OFF:
        up, low = entry(a, b), entry(b, a)
        out += [up[0] - low[0], up[1] + low[1]]
    return out


def anti_mm(x, y):
    def imag(a, b):
        terms = [x[a][c][0] * y[c][b][1] + x[a][c][1] * y[c][b][0] for c in R3]
        return terms[0] + terms[1] + terms[2]

    return anti(lambda a, b: total([cmul(x[a][c], y[c][b]) for c in R3]), imag)


def anti_mm_h(x, y):
    def imag(a, b):
        terms = [x[a][c][1] * y[b][c][0] - x[a][c][0] * y[b][c][1] for c in R3]
        return terms[0] + terms[1] + terms[2]

    return anti(lambda a, b: total([mul_conj(x[a][c], y[b][c]) for c in R3]), imag)


def exp_series(w):
    mean = (w[0] + w[1] + w[2]) * (RHO / 3.0)
    h = [w[a] * RHO - mean for a in R3]
    z = {}
    for at, (a, b) in enumerate(OFF):
        z[a, b] = (w[3 + 2 * at] * (0.5 * RHO), w[4 + 2 * at] * (0.5 * RHO))
    size = {ab: v[0] * v[0] + v[1] * v[1] for ab, v in z.items()}
    s_diag = [
        -(h[0] * h[0] + size[0, 1] + size[0, 2]),
        -(h[1] * h[1] + size[0, 1] + size[1, 2]),
        -(h[2] * h[2] + size[0, 2] + size[1, 2]),
    ]

    def turned(v, by):
        return (-by * v[1], by * v[0])

    neg = lambda v: (-v[0], -v[1])
    s = {
        (0, 1): cadd(turned(z[0, 1], h[0] + h[1]), neg(mul_conj(z[0, 2], z[1, 2]))),
        (0, 2): cadd(turned(z[0, 2], h[0] + h[2]), cmul(z[0, 1], z[1, 2])),
        (1, 2): cadd(turned(z[1, 2], h[1] + h[2]), neg(conj_mul(z[0, 1], z[0, 2]))),
    }
    p = 0.5 * (s_diag[0] + s_diag[1] + s_diag[2])
    ha, hb, hc = [(z[ab][1], -z[ab][0]) for ab in OFF]
    triple = cmul(ha, hc)
    det = (
        h[0] * (h[1] * h[2] - size[1, 2])
        - h[1] * size[0, 2]
        - h[2] * size[0, 1]
        + 2.0 * (triple[0] * hb[0] + triple[1] * hb[1])
    )
    k = -det
    f0 = (1.0 - (k * (1.0 / 720.0)) * k, k * (1.0 / 6.0 + p * (1.0 / 120.0)))
    f1 = (1.0 + p * (1.0 / 6.0) + (p * (1.0 / 120.0)) * p, k * (1.0 / 24.0 + p * (1.0 / 360.0)))
    f2 = (0.5 + p * (1.0 / 24.0) + (p * (1.0 / 720.0)) * p, k * (1.0 / 120.0))
    out = [[None] * 3 for _ in R3]
    for a in R3:
        out[a][a] = (
            f0[0] - f1[1] * h[a] + f2[0] * s_diag[a],
            f0[1] + f1[0] * h[a] + f2[1] * s_diag[a],
        )
    for a, b in OFF:
        (zr, zi), (sr, si) = z[a, b], s[a, b]
        rr, ri, ir, ii = f1[0] * zr, f1[0] * zi, f1[1] * zr, f1[1] * zi
        tr, ti, ur, ui = f2[0] * sr, f2[0] * si, f2[1] * sr, f2[1] * si
        out[a][b] = (rr - ii + tr - ui, ri + ir + ti + ur)
        out[b][a] = (tr + ui - rr - ii, ri - ir + ur - ti)
    return out


def pack_kernel(pos, links, links_in, chip, edge_up, edge_down):
    second = (pos[0] & 1) == 1
    half = links.shape[1]
    a, b = links[...], links_in[...]
    planes = (jnp.where(second, b, a), jnp.where(second, a, b))
    high = [v.astype(BF16) for v in planes]
    low = [(v - h.astype(F32)).astype(BF16) for v, h in zip(planes, high)]
    for at in range(2):
        chip[:, half * at : half * (at + 1), :] = planes[at]
    for out, parts in ((edge_up, high + [low[1]]), (edge_down, high + [low[0]])):
        for at, v in enumerate(parts):
            out[:, half * at : half * (at + 1), :] = v


def smear_kernel(below, own, above, out, links, moved):
    rows = own.shape[1] // 2
    low, high = below[...].astype(F32), above[...].astype(F32)
    parts = (
        low[:, :rows],
        low[:, rows : 2 * rows] + low[:, 2 * rows :],
        own[:, :rows],
        own[:, rows:],
        high[:, :rows] + high[:, 2 * rows :],
        high[:, rows : 2 * rows],
    )
    for at, part in enumerate(parts):
        links[0, :, rows * at : rows * (at + 1), :] = part
    tile = 4 * rows
    lane = lax.broadcasted_iota(jnp.int32, (tile, 128), 1)
    row = lax.broadcasted_iota(jnp.int32, (tile, 128), 0)
    even = (row & 1) == 0
    z_at = lane & (LZ - 1)

    def flip(x):
        return jnp.where(even, pltpu.roll(x, tile - 1, 0), pltpu.roll(x, 1, 0))

    def ahead_y(x):
        x = pltpu.roll(x, 128 - LZ, 1)
        return jnp.where(lane < 128 - LZ, x, flip(x))

    def behind_y(x):
        x = pltpu.roll(x, LZ, 1)
        return jnp.where(lane >= LZ, x, flip(x))

    def ahead_z(x):
        return jnp.where(z_at < LZ - 1, pltpu.roll(x, 127, 1), pltpu.roll(x, LZ - 1, 1))

    def behind_z(x):
        return jnp.where(z_at > 0, pltpu.roll(x, 1, 1), pltpu.roll(x, 128 - LZ + 1, 1))

    moved[...] = jnp.zeros_like(moved)

    def step(j, carry):
        source = jnp.where(j == 2, 1, 0)
        base = jnp.where(j == 2, rows, tile * j)
        target = jnp.where(j == 2, 2, 1)
        write = jnp.where(j == 2, 0, tile * j)
        base = pl.multiple_of(base, rows)
        write = pl.multiple_of(write, rows)

        def raw(c, off=0):
            return links[source, c, pl.ds(base + off, tile), :]

        def matrix(m, move=None, off=0):
            move = move or (lambda v: v)
            at = lambda a, b, r: move(raw(18 * m + 2 * (3 * a + b) + r, off))
            return [[(at(a, b, 0), at(a, b, 1)) for b in R3] for a in R3]

        def ahead(m, n):
            if n == 0:
                return matrix(m, None, rows)
            return matrix(m, ahead_y if n == 1 else ahead_z)

        def behind(values, n, slot):
            if n == 1:
                return [behind_y(v) for v in values]
            if n == 2:
                return [behind_z(v) for v in values]
            back = []
            for c, v in enumerate(values):
                moved[source, 9 * slot + c, pl.ds(base + rows, tile), :] = v
                back.append(moved[source, 9 * slot + c, pl.ds(base, tile), :])
            return back

        w = [None, None, None]

        def give(m, values, sign):
            if w[m] is None:
                assert sign > 0
                w[m] = values
            else:
                w[m] = [a + b if sign > 0 else a - b for a, b in zip(w[m], values)]

        for m, n in ((0, 1), (2, 0), (1, 2)):
            um, un = matrix(m), matrix(n)
            y = mm_h(ahead(n, m), ahead(m, n))
            x = h_mm(un, um)
            plaq = anti_mm_h(mm_h(un, y), um)
            give(m, plaq, 1)
            q_m = anti_mm(x, y)
            q_n = anti_mm(y, x)
            slot = 0 if 1 in (m, n) else 1
            give(m, behind(q_m, n, slot), 1)
            if w[n] is None:
                w[n] = [-a for a in plaq]
            else:
                give(n, plaq, -1)
            give(n, behind(q_n, m, slot), -1)
        for m in R3:
            new = mm(exp_series(w[m]), matrix(m))
            for a in R3:
                for b in R3:
                    for r in range(2):
                        c = 18 * m + 2 * (3 * a + b) + r
                        links[target, c, pl.ds(write, tile), :] = new[a][b][r]
        return carry

    lax.fori_loop(0, 3, step, 0)
    out[...] = links[2, :, rows : 3 * rows, :]


def split_links_kernel(pos, links, keep, send, links_v, sem):
    second = (pos[0] & 1) == 1
    rows = keep.shape[1]
    copy = pltpu.make_async_copy(links, links_v, sem)
    copy.start()
    copy.wait()
    a, b = links_v[:, :rows], links_v[:, rows:]
    keep[...] = jnp.where(second, b, a)
    send[...] = jnp.where(second, a, b)


def order_kernel(pos, vectors, pair, order, momenta, pairs, ordered, first, momenta_out, index, *scratch):
    vectors_v, ordering, pairs_v, sems = scratch
    nt, comps, count, sites = vectors.shape
    t = pos[0] & (nt - 1)
    up = pos[0] & 1
    copies = [
        pltpu.make_async_copy(vectors.at[t], vectors_v.at[up], sems.at[0]),
        pltpu.make_async_copy(pair.at[t], vectors_v.at[1 - up], sems.at[1]),
        pltpu.make_async_copy(order, ordering, sems.at[2]),
        pltpu.make_async_copy(momenta, momenta_out, sems.at[3]),
        pltpu.make_async_copy(pairs, pairs_v, sems.at[4]),
    ]
    for copy in copies:
        copy.start()
    row = lax.broadcasted_iota(jnp.int32, (count, count), 0)
    for copy in copies:
        copy.wait()
    low = jnp.minimum(pairs_v[0:1, :], pairs_v[1:2, :])
    high = jnp.maximum(pairs_v[0:1, :], pairs_v[1:2, :])
    index[...] = low * nt - (low * (low - 1)) // 2 + (high - low)
    hot = jnp.where(row == ordering[pl.ds(t, 1), :], 1.0, 0.0).T.astype(BF16)
    for p in range(2):
        for c in range(comps):
            picked = jnp.dot(hot, vectors_v[p, c], preferred_element_type=F32).astype(BF16)
            m, r = c // 2, c % 2
            rows, cols = slice(r * count, (r + 1) * count), slice(m * sites, (m + 1) * sites)
            ordered[p, rows, cols] = picked
            if p == 0:
                first[rows, cols] = picked


def move_kernel(total_x, pos, momenta, ordered, out_y, out_z, phase):
    planes, _, width = ordered.shape
    sites = width // 3
    src = lax.broadcasted_iota(jnp.int32, (sites, sites), 0)
    dst = lax.broadcasted_iota(jnp.int32, (sites, sites), 1)
    to_y = (dst + LZ) & (sites - 1)
    to_z = jnp.where((dst & (LZ - 1)) < LZ - 1, dst + 1, dst - (LZ - 1))
    for out, to in ((out_y, to_y), (out_z, to_z)):
        hot = jnp.where(src == to, 1.0, 0.0).astype(BF16)
        for p in range(planes):
            for a in range(3):
                at = slice(a * sites, (a + 1) * sites)
                out[p, :, at] = jnp.dot(
                    ordered[p, :, at], hot, preferred_element_type=F32
                ).astype(BF16)
    nops = momenta.shape[0]
    shape = (4 * nops, 128)
    row = lax.broadcasted_iota(jnp.int32, shape, 0)
    site = (row & 1) * 128 + lax.broadcasted_iota(jnp.int32, shape, 1)
    x_at = (pos[0] >> 1) * 2 + ((row >> 1) & 1)
    y_at, z_at = site // LZ, site & (LZ - 1)
    period = total_x * LY * LZ
    number = jnp.zeros(shape, jnp.int32)
    for k in range(nops):
        here = (
            momenta[k : k + 1, 0:1] * x_at * (LY * LZ)
            + momenta[k : k + 1, 1:2] * y_at * (total_x * LZ)
            + momenta[k : k + 1, 2:3] * z_at * (total_x * LY)
        )
        number = jnp.where((row >> 2) == k, here, number)
    number = number & (period - 1)
    quarter = period // 4
    turn = (number + quarter // 2) // quarter
    angle = (number - turn * quarter).astype(F32) * (2.0 * math.pi / period)
    sq = angle * angle
    sin = 1.0 / 362880.0
    for d in (-5040.0, 120.0, -6.0, 1.0):
        sin = sin * sq + 1.0 / d
    sin = sin * angle
    cos = -1.0 / 3628800.0
    for d in (40320.0, -720.0, 24.0, -2.0, 1.0):
        cos = cos * sq + 1.0 / d
    turn = turn & 3
    odd = (turn & 1) == 1
    big, small = jnp.where(odd, sin, cos), jnp.where(odd, cos, sin)
    phase[0] = jnp.where((turn == 1) | (turn == 2), -big, big)
    phase[1] = -jnp.where(turn >= 2, -small, small)


def elemental_kernel(scale, ops, pos, links, phase, ordered, *refs):
    nears, (send, keep, right) = refs[:-3], refs[-3:]
    planes, rows, width = ordered.shape
    count, sites = rows // 2, width // 3
    up = (pos[0] >> 1) & 1
    sub = 16
    grams = []
    for at, k in enumerate(ops):
        m = k % 3
        near = nears[at % len(nears)] if m else None
        gram = None
        for p in range(planes):
            for h in range(2):
                pr, pi = (phase[r, 4 * k + 2 * p + h : 4 * k + 2 * p + h + 1, :] for r in range(2))
                coef = []
                for e in range(9):
                    c = 18 * m + 2 * e
                    cr, ci = (links[c + r, 2 * p + h : 2 * p + h + 1, :] for r in range(2))
                    both = (pr * cr - pi * ci, pr * ci + pi * cr)
                    coef.append([jnp.broadcast_to(v, (sub, 128)) for v in both])
                for i in range(count // sub):
                    v = []
                    for b in range(3):
                        lo = b * sites + h * 128
                        cols = slice(lo, lo + 128)
                        parts = []
                        for r in range(2):
                            at_rows = slice(r * count + i * sub, r * count + (i + 1) * sub)
                            if m:
                                got = near[p, at_rows, cols]
                            elif p + 1 < planes:
                                got = ordered[p + 1, at_rows, cols]
                            else:
                                got = nears[0][at_rows, cols]
                            parts.append(got.astype(F32))
                        v.append(parts)
                    for a in range(3):
                        got = total([cmul(coef[3 * a + b], v[b]) for b in range(3)])
                        lo = a * sites + h * 128
                        for r in range(2):
                            at_rows = slice(r * count + i * sub, r * count + (i + 1) * sub)
                            right[at, p, at_rows, lo : lo + 128] = got[r].astype(BF16)
            part = lax.dot_general(
                ordered[p], right[at, p], (((1,), (1,)), ((), ())), preferred_element_type=F32
            )
            gram = part if gram is None else gram + part
        grams.append(
            (
                (gram[:count, :count] + gram[count:, count:]) * scale,
                (gram[:count, count:] - gram[count:, :count]) * scale,
            )
        )
    for r in range(2):
        first, second = grams[0][r], grams[1][r]
        send[r] = jnp.where(up == 1, first, second).astype(send.dtype)
        keep[r] = jnp.where(up == 1, second, first)


def split_kernel(pos, early, early_in, late, late_in, send, keep):
    up = ((pos[0] >> 2) & 1) == 1
    a = early[...] + early_in[...].astype(F32)
    b = late[...] + late_in[...].astype(F32)
    send[...] = jnp.where(up, a, b).astype(send.dtype)
    keep[...] = jnp.where(up, b, a)


def add_kernel(mine, other, out):
    out[...] = (mine[...].astype(F32) + other[...].astype(F32)).astype(out.dtype)


def trace_kernel(pos, mine, other, mine_b, other_b, tau, *outs):
    nt, count = tau.shape[0], tau.shape[-1]
    parity = pos[0] & (nt - 1)
    per, ib = mine_b.shape[1], mine_b.shape[2]
    for at, out in enumerate(outs):
        d = pos[0] ^ (2 * at)
        a, b = mine_b[:, d % per], other_b[:, d % per]
        picked = jnp.where((d // per) == parity, a, b)
        for r in range(2):
            out[r * ib : (r + 1) * ib, :] = picked[r]
    phi = []
    for t in range(nt):
        own, oth = mine[...], other[...]
        x = jnp.where(parity == t, own, oth).reshape(2 * count, count)
        hi = x.astype(BF16)
        lo = (x - hi.astype(F32)).astype(BF16)
        phi.append(jnp.concatenate([hi, lo], axis=0))
    prod = {}
    for t in range(nt):
        for u in range(nt):
            right = jnp.concatenate([tau[t, u, 0], tau[t, u, 1]], axis=1)
            got = jnp.dot(phi[t], right, preferred_element_type=F32)
            got = got[: 2 * count] + got[2 * count :]
            prod[t, u] = (
                got[:count, :count] - got[count:, count:],
                got[:count, count:] + got[count:, :count],
            )
    rows = []
    for t in range(nt):
        for u in range(t, nt):
            xr, xi = prod[t, u]
            yr, yi = prod[u, t][0].T, prod[u, t][1].T
            rows.append(jnp.sum(xr * yr - xi * yi, axis=0, keepdims=True))
            rows.append(jnp.sum(xr * yi + xi * yr, axis=0, keepdims=True))
    base = 2 * ib
    for out in outs:
        for at, v in enumerate(rows):
            out[base + at : base + at + 1, :] = v
        out[base + len(rows) :, :] = jnp.zeros_like(out[base + len(rows) :, :])


def final_kernel(ib, pos, chosen, *refs):
    parts, (out, corr) = [ref[...] for ref in refs[:4]], refs[4:]
    at = (pos[0] >> 1) & 3
    index = chosen[...]
    combos = (parts[0].shape[0] - 2 * ib) // 2
    for k in range(4):
        home = (2, 0, 1, 3)[k]
        v = parts[0]
        for flip in range(1, 4):
            v = jnp.where((at ^ flip) == home, parts[flip], v)
        for r in range(2):
            out[k, pl.ds(r, ib, stride=2), :] = v[r * ib : (r + 1) * ib]
        sums = jnp.sum(v[2 * ib :], axis=1, keepdims=True)
        for r in range(2):
            line = jnp.zeros(index.shape, F32)
            for j in range(combos):
                value = jnp.broadcast_to(sums[2 * j + r : 2 * j + r + 1, :], index.shape)
                line = jnp.where(index == j, value, line)
            corr[k, r : r + 1, :] = line


def on_device(vectors, gauge_links, perambulators, time_pairs, ordering, op_momenta):
    devices = lax.axis_size("space")
    pos = lax.axis_index("space").astype(jnp.int32).reshape(1)
    nt, count, comps, planes, sites = vectors.shape
    nops = op_momenta.shape[0]
    total_x = planes * devices
    assert planes == 1 and nt == 2 and nops == 4 and devices >= 8
    assert devices & (devices - 1) == 0 and sites == LY * LZ == 256
    scale = (3.0 * total_x * LY * LZ) ** (-0.5)

    natural = jnp.transpose(vectors, (0, 2, 3, 1, 4)).reshape(nt, comps, count, sites)
    own = gauge_links.reshape(54, nt * 2, 128)
    rows = 4
    wide = (2, 2 * count, 3 * sites)
    half = (54, rows // 2, 128)
    links_keep, links_send = call(
        split_links_kernel,
        [(half, F32), (half, F32)],
        [pos, own],
        scalars=1,
        loose=1,
        scratch=[pltpu.VMEM((54, rows, 128), F32), pltpu.SemaphoreType.DMA],
    )
    edge = ((54, 3 * rows // 2, 128), BF16)
    chip_links, edge_up, edge_down = call(
        pack_kernel,
        [((54, rows, 128), F32), edge, edge],
        [pos, links_keep, swapped(links_send, 1)],
        scalars=1,
    )
    below, above = shifted(edge_up, 2), shifted(edge_down, -2)
    npair = time_pairs.shape[0]
    ordered, first, momenta, chosen = call(
        order_kernel,
        [(wide, BF16), (wide[1:], BF16), (op_momenta.shape, jnp.int32), ((1, npair), jnp.int32)],
        [pos, natural, swapped(natural, 1), ordering, op_momenta, time_pairs.T],
        scalars=1,
        loose=5,
        scratch=[
            pltpu.VMEM((2, comps, count, sites), BF16),
            pltpu.VMEM((nt, count), jnp.int32),
            pltpu.VMEM((2, npair), jnp.int32),
            pltpu.SemaphoreType.DMA((5,)),
        ],
    )
    near_x = shifted(first, -2)
    near_y, near_z, phase = call(
        lambda *refs: move_kernel(total_x, *refs),
        [(wide, BF16), (wide, BF16), ((2, 4 * nops, 128), F32)],
        [pos, momenta, ordered],
        scalars=1,
    )
    (smeared,) = call(
        smear_kernel,
        [((54, rows, 128), F32)],
        [below, chip_links, above],
        scratch=[pltpu.VMEM((3, 54, 24, 128), F32), pltpu.VMEM((2, 18, 24, 128), F32)],
    )
    flat = (2, count, count)

    def grams(ops, nears, kind):
        return call(
            lambda *refs: elemental_kernel(scale, ops, *refs),
            [(flat, kind), (flat, F32)],
            [pos, smeared, phase, ordered] + nears,
            scalars=1,
            scratch=[pltpu.VMEM((2,) + wide, BF16)],
        )

    send, early = grams((1, 2), [near_y, near_z], F32)
    early_in = swapped(send, 2)
    send, late = grams((0, 3), [near_x], BF16)
    late_in = swapped(send, 2)
    send, keep = call(
        split_kernel, [(flat, F32), (flat, F32)], [pos, early, early_in, late, late_in], scalars=1
    )
    bit = 8
    other = swapped(send, 4)
    while bit <= devices:
        (keep,) = call(add_kernel, [(flat, BF16 if bit < devices else F32)], [keep, other])
        other = swapped(keep, bit if bit < devices else 1)
        bit *= 2
    mine = keep
    ib = nt * count // devices
    per = devices // nt
    blocks = call(
        trace_kernel,
        [((2 * ib + 8, 128), F32)] * 4,
        [
            pos,
            mine,
            other,
            mine.reshape(2, per, ib, count),
            other.reshape(2, per, ib, count),
            perambulators,
        ],
        scalars=1,
    )
    parts = [blocks[0]] + [swapped(blocks[f], 2 * f) for f in range(1, 4)]
    out, corr = call(
        lambda *refs: final_kernel(ib, *refs),
        [((nops, 2 * ib, count), F32), ((nops, 2, npair), F32)],
        [pos, chosen] + parts,
        scalars=1,
    )
    return out, jnp.transpose(corr, (0, 2, 1))


def solution(mesh):
    return jax.shard_map(
        on_device,
        mesh=mesh,
        in_specs=(
            P("grp", None, None, "space", None),
            P(None, None, "grp", "space", None),
            P("grp", None, None, None, None),
            P("grp", None),
            P("grp", None),
            P(),
        ),
        out_specs=(P("grp", "space", None), P("grp", None, None)),
        check_vma=False,
    )
```

profile of v0, /device:TPU:0, one launch (start us, length us, event | category | flops | bytes accessed | tf_op | source)
XLA Modules:
  0.0 58.2 jit_solution(9092673770546717920)
XLA Ops:
  0.6 0.6 collective-permute-start
  1.2 2.1 %collective-permute-done.pair = bf16[2,6,128,256]{3,2,1,0:T(8,128)(2,1)S(1)} collective-permute-done((bf16[2,6,128,256]{3,2,1,0:T(8,128)(2,1)}, bf16[2,6,128,256]{3,2,1,0:T(8,128)(2,1)S(1)}, u32[]{:S(2)}, u32[]{:S(2)}) %collective-permute-start) | collective-permute-done | bytes 786464 | tf_op jit(solution)/shard_map/ppermute | solution.py:52
  3.3 0.0 copy-start.1
  3.3 0.9 %copy-done.1 = bf16[2,6,128,256]{3,2,1,0:T(8,128)(2,1)} copy-done((bf16[2,6,128,256]{3,2,1,0:T(8,128)(2,1)}, bf16[2,6,128,256]{3,2,1,0:T(8,128)(2,1)S(1)}, u32[]{:S(2)}) %copy-start.1) | copy-done | bytes 786456
  4.2 1.6 %shard_map.77 = (bf16[2,256,768]{2,1,0:T(8,128)(2,1)S(1)}, bf16[256,768]{1,0:T(8,128)(2,1)S(1)}, s32[4,3]{1,0:T(4,128)S(1)}, s32[1,8]{1,0:T(1,128)S(1)}) custom-call(s32[1]{0:T(128)} %bitcast.pos.refs_0_, bf16[2,6,128,256]{3,2,1,0:T(8,128)(2,1)} %bitcast.14, bf16[2,6,128,256]{3,2,1,0:T(8,128)(2,1)} %copy-done.1, s32[2,128]{1,0:T(2,128)} %order.1, ...), custom_call_target="tpu_custom_call" | custom-call | flops 1000000 | bytes 1000000 | tf_op jit(solution)/shard_map/pallas_call | solution.py:42
  5.8 6.0 %collective-permute-start.5 = (bf16[256,768]{1,0:T(8,128)(2,1)S(1)}, bf16[256,768]{1,0:T(8,128)(2,1)S(1)}, u32[]{:S(2)}, u32[]{:S(2)}) collective-permute-start(bf16[256,768]{1,0:T(8,128)(2,1)S(1)} %get-tuple-element.39), channel_id=1, source_target_pairs={{0,14},{1,15},{2,0},{3,1},{4,2},{5,3},{6,4},{7,5},{8,6},{9,7},{10,... | collective-permute-start | bytes 1179656 | tf_op jit(solution)/shard_map/ppermute | solution.py:47
  11.7 0.9 %shard_map.78 = (f32[54,2,128]{2,1,0:T(2,128)S(1)}, f32[54,2,128]{2,1,0:T(2,128)S(1)}) custom-call(s32[1]{0:T(128)} %bitcast.pos.refs_0_, f32[54,4,128]{2,1,0:T(4,128)} %bitcast.15), custom_call_target="tpu_custom_call" | custom-call | flops 1000000 | bytes 1000000 | tf_op jit(solution)/shard_map/pallas_call | solution.py:42
  12.7 0.1 collective-permute-start.1
  12.8 1.2 %collective-permute-done.1.links_in = f32[54,2,128]{2,1,0:T(2,128)S(1)} collective-permute-done((f32[54,2,128]{2,1,0:T(2,128)S(1)}, f32[54,2,128]{2,1,0:T(2,128)S(1)}, u32[]{:S(2)}, u32[]{:S(2)}) %collective-permute-start.1) | collective-permute-done | bytes 55328 | tf_op jit(solution)/shard_map/ppermute | solution.py:52
  14.0 0.2 shard_map.79
  14.2 0.1 collective-permute-start.2
  14.3 4.7 %collective-permute-start.3 = (bf16[54,6,128]{2,1,0:T(8,128)(2,1)S(1)}, bf16[54,6,128]{2,1,0:T(8,128)(2,1)S(1)}, u32[]{:S(2)}, u32[]{:S(2)}) collective-permute-start(bf16[54,6,128]{2,1,0:T(8,128)(2,1)S(1)} %get-tuple-element.31), channel_id=1, source_target_pairs={{0,14},{1,15},{2,0},{3,1},{4,2},{5,3},{6,4},{7,5},{8,6},{9,7},{10,... | collective-permute-start | bytes 248840 | tf_op jit(solution)/shard_map/ppermute | solution.py:47
  19.0 4.1 %collective-permute-done.2.below = bf16[54,6,128]{2,1,0:T(8,128)(2,1)S(1)} collective-permute-done((bf16[54,6,128]{2,1,0:T(8,128)(2,1)S(1)}, bf16[54,6,128]{2,1,0:T(8,128)(2,1)S(1)}, u32[]{:S(2)}, u32[]{:S(2)}) %collective-permute-start.2) | collective-permute-done | bytes 82976 | tf_op jit(solution)/shard_map/ppermute | solution.py:47
  23.0 0.0 collective-permute-done.3.above
  23.0 2.3 %shard_map.80.refs_1_ = f32[54,4,128]{2,1,0:T(4,128)S(1)} custom-call(bf16[54,6,128]{2,1,0:T(8,128)(2,1)S(1)} %collective-permute-done.2.below, f32[54,4,128]{2,1,0:T(4,128)S(1)} %get-tuple-element.30.own, bf16[54,6,128]{2,1,0:T(8,128)(2,1)S(1)} %collective-permute-done.3.above), custom_call_target="tpu_custom_call" | custom-call | flops 1000000 | bytes 1000000 | tf_op jit(solution)/shard_map/pallas_call | solution.py:42
  25.4 0.6 %shard_map.81 = (bf16[2,256,768]{2,1,0:T(8,128)(2,1)S(1)}, bf16[2,256,768]{2,1,0:T(8,128)(2,1)S(1)}, f32[2,16,128]{2,1,0:T(8,128)S(1)}) custom-call(s32[1]{0:T(128)} %bitcast.pos.refs_0_, s32[4,3]{1,0:T(4,128)S(1)} %get-tuple-element.32.refs_1_, bf16[2,256,768]{2,1,0:T(8,128)(2,1)S(1)} %get-tuple-element.33.refs_2_.refs_3_), custom_call_target="tpu_custom_call" | custom-call | flops 1000000 | bytes 1000000 | tf_op jit(solution)/shard_map/pallas_call | solution.py:42
  26.0 2.0 %shard_map.82 = (f32[2,128,128]{2,1,0:T(8,128)S(1)}, f32[2,128,128]{2,1,0:T(8,128)S(1)}) custom-call(s32[1]{0:T(128)} %bitcast.pos.refs_0_, f32[54,4,128]{2,1,0:T(4,128)S(1)} %shard_map.80.refs_1_, f32[2,16,128]{2,1,0:T(8,128)S(1)} %get-tuple-element.34.refs_2_, bf16[2,256,768]{2,1,0:T(8,128)(2,1)S(1)} %get-tuple-element.33.refs_2_.refs_3_, ...), custom_call_target="tpu_custom_call" | custom-call | flops 1000000 | bytes 1000000 | tf_op jit(solution)/shard_map/pallas_call | solution.py:42
  28.0 2.5 %collective-permute-start.4 = (f32[2,128,128]{2,1,0:T(8,128)S(1)}, f32[2,128,128]{2,1,0:T(8,128)S(1)}, u32[]{:S(2)}, u32[]{:S(2)}) collective-permute-start(f32[2,128,128]{2,1,0:T(8,128)S(1)} %get-tuple-element.38), channel_id=1, source_target_pairs={{0,2},{1,3},{2,0},{3,1},{4,6},{5,7},{6,4},{7,5},{8,10},{9,11},{10,... | collective-permute-start | bytes 393224 | tf_op jit(solution)/shard_map/ppermute | solution.py:52
  30.6 0.0 collective-permute-done.5.refs_4_
  30.6 2.0 %shard_map.83 = (bf16[2,128,128]{2,1,0:T(8,128)(2,1)S(1)}, f32[2,128,128]{2,1,0:T(8,128)S(1)}) custom-call(s32[1]{0:T(128)} %bitcast.pos.refs_0_, f32[54,4,128]{2,1,0:T(4,128)S(1)} %shard_map.80.refs_1_, f32[2,16,128]{2,1,0:T(8,128)S(1)} %get-tuple-element.34.refs_2_, bf16[2,256,768]{2,1,0:T(8,128)(2,1)S(1)} %get-tuple-element.33.refs_2_.refs_3_, ...), custom_call_target="tpu_custom_call" | custom-call | flops 1000000 | bytes 1000000 | tf_op jit(solution)/shard_map/pallas_call | solution.py:42
  32.5 0.1 collective-permute-start.6
  32.6 1.6 %collective-permute-done.4.early_in = f32[2,128,128]{2,1,0:T(8,128)S(1)} collective-permute-done((f32[2,128,128]{2,1,0:T(8,128)S(1)}, f32[2,128,128]{2,1,0:T(8,128)S(1)}, u32[]{:S(2)}, u32[]{:S(2)}) %collective-permute-start.4) | collective-permute-done | bytes 131104 | tf_op jit(solution)/shard_map/ppermute | solution.py:52
  34.3 2.6 %collective-permute-done.6.late_in = bf16[2,128,128]{2,1,0:T(8,128)(2,1)S(1)} collective-permute-done((bf16[2,128,128]{2,1,0:T(8,128)(2,1)S(1)}, bf16[2,128,128]{2,1,0:T(8,128)(2,1)S(1)}, u32[]{:S(2)}, u32[]{:S(2)}) %collective-permute-start.6) | collective-permute-done | bytes 65568 | tf_op jit(solution)/shard_map/ppermute | solution.py:52
  36.9 1.6 %collective-permute-start.7 = (f32[2,128,128]{2,1,0:T(8,128)S(1)}, f32[2,128,128]{2,1,0:T(8,128)S(1)}, u32[]{:S(2)}, u32[]{:S(2)}) collective-permute-start(f32[2,128,128]{2,1,0:T(8,128)S(1)} %get-tuple-element.43), channel_id=1, source_target_pairs={{0,4},{1,5},{2,6},{3,7},{4,0},{5,1},{6,2},{7,3},{8,12},{9,13},{10,... | collective-permute-start | bytes 393224 | tf_op jit(solution)/shard_map/ppermute | solution.py:52
  38.6 3.4 %collective-permute-done.7.other = f32[2,128,128]{2,1,0:T(8,128)S(1)} collective-permute-done((f32[2,128,128]{2,1,0:T(8,128)S(1)}, f32[2,128,128]{2,1,0:T(8,128)S(1)}, u32[]{:S(2)}, u32[]{:S(2)}) %collective-permute-start.7) | collective-permute-done | bytes 131104 | tf_op jit(solution)/shard_map/ppermute | solution.py:52
  41.9 0.0 copy-start
  42.0 4.0 %collective-permute-start.8 = (bf16[2,128,128]{2,1,0:T(8,128)(2,1)S(1)}, bf16[2,128,128]{2,1,0:T(8,128)(2,1)S(1)}, u32[]{:S(2)}, u32[]{:S(2)}) collective-permute-start(bf16[2,128,128]{2,1,0:T(8,128)(2,1)S(1)} %shard_map.85.mine), channel_id=1, source_target_pairs={{0,8},{1,9},{2,10},{3,11},{4,12},{5,13},{6,14},{7,15},{8,0},{9,1},... | collective-permute-start | bytes 196616 | tf_op jit(solution)/shard_map/ppermute | solution.py:52
  46.0 2.2 %collective-permute-done.8.other = bf16[2,128,128]{2,1,0:T(8,128)(2,1)S(1)} collective-permute-done((bf16[2,128,128]{2,1,0:T(8,128)(2,1)S(1)}, bf16[2,128,128]{2,1,0:T(8,128)(2,1)S(1)}, u32[]{:S(2)}, u32[]{:S(2)}) %collective-permute-start.8) | collective-permute-done | bytes 65568 | tf_op jit(solution)/shard_map/ppermute | solution.py:52
  48.2 0.1 collective-permute-start.9
  48.3 1.3 %collective-permute-done.9.other = f32[2,128,128]{2,1,0:T(8,128)S(1)} collective-permute-done((f32[2,128,128]{2,1,0:T(8,128)S(1)}, f32[2,128,128]{2,1,0:T(8,128)S(1)}, u32[]{:S(2)}, u32[]{:S(2)}) %collective-permute-start.9) | collective-permute-done | bytes 131104 | tf_op jit(solution)/shard_map/ppermute | solution.py:52
  49.7 0.0 copy-done
  49.7 0.5 shard_map.87
  50.2 0.7 %collective-permute-start.10 = (f32[40,128]{1,0:T(8,128)S(1)}, f32[40,128]{1,0:T(8,128)S(1)}, u32[]{:S(2)}, u32[]{:S(2)}) collective-permute-start(f32[40,128]{1,0:T(8,128)S(1)} %get-tuple-element.45), channel_id=1, source_target_pairs={{0,2},{1,3},{2,0},{3,1},{4,6},{5,7},{6,4},{7,5},{8,10},{9,11},{10,... | collective-permute-start | bytes 61448 | tf_op jit(solution)/shard_map/ppermute | solution.py:52
  50.9 1.9 %collective-permute-start.11 = (f32[40,128]{1,0:T(8,128)S(1)}, f32[40,128]{1,0:T(8,128)S(1)}, u32[]{:S(2)}, u32[]{:S(2)}) collective-permute-start(f32[40,128]{1,0:T(8,128)S(1)} %get-tuple-element.46), channel_id=1, source_target_pairs={{0,4},{1,5},{2,6},{3,7},{4,0},{5,1},{6,2},{7,3},{8,12},{9,13},{10,... | collective-permute-start | bytes 61448 | tf_op jit(solution)/shard_map/ppermute | solution.py:52
  52.8 0.9 %collective-permute-start.12 = (f32[40,128]{1,0:T(8,128)S(1)}, f32[40,128]{1,0:T(8,128)S(1)}, u32[]{:S(2)}, u32[]{:S(2)}) collective-permute-start(f32[40,128]{1,0:T(8,128)S(1)} %get-tuple-element.47), channel_id=1, source_target_pairs={{0,6},{1,7},{2,4},{3,5},{4,2},{5,3},{6,0},{7,1},{8,14},{9,15},{10,... | collective-permute-start | bytes 61448 | tf_op jit(solution)/shard_map/ppermute | solution.py:52
  53.7 0.3 collective-permute-done.10.refs_3_
  54.0 0.6 %collective-permute-done.11.refs_4_ = f32[40,128]{1,0:T(8,128)S(1)} collective-permute-done((f32[40,128]{1,0:T(8,128)S(1)}, f32[40,128]{1,0:T(8,128)S(1)}, u32[]{:S(2)}, u32[]{:S(2)}) %collective-permute-start.11) | collective-permute-done | bytes 20512 | tf_op jit(solution)/shard_map/ppermute | solution.py:52
  54.7 2.8 %collective-permute-done.12.refs_5_ = f32[40,128]{1,0:T(8,128)S(1)} collective-permute-done((f32[40,128]{1,0:T(8,128)S(1)}, f32[40,128]{1,0:T(8,128)S(1)}, u32[]{:S(2)}, u32[]{:S(2)}) %collective-permute-start.12) | collective-permute-done | bytes 20512 | tf_op jit(solution)/shard_map/ppermute | solution.py:52
  57.5 0.7 %shard_map.88 = (f32[4,32,128]{2,1,0:T(8,128)}, f32[4,2,8]{2,1,0:T(2,128)}) custom-call(s32[1]{0:T(128)} %bitcast.pos.refs_0_, s32[1,8]{1,0:T(1,128)S(1)} %get-tuple-element.26.refs_1_, f32[40,128]{1,0:T(8,128)S(1)} %get-tuple-element.44.refs_2_, f32[40,128]{1,0:T(8,128)S(1)} %collective-permute-done.10.refs_3_, ...), custom_call_target="tpu_custom_call" | custom-call | flops 1000000 | bytes 1000000 | tf_op jit(solution)/shard_map/pallas_call | solution.py:42
  (3 shorter events, 0.1 us)
Async XLA Ops:
  0.6 2.7 %collective-permute-start = (bf16[2,6,128,256]{3,2,1,0:T(8,128)(2,1)}, bf16[2,6,128,256]{3,2,1,0:T(8,128)(2,1)S(1)}, u32[]{:S(2)}, u32[]{:S(2)}) collective-permute-start(bf16[2,6,128,256]{3,2,1,0:T(8,128)(2,1)} %bitcast.13), channel_id=1, source_target_pairs={{0,1},{1,0},{2,3},{3,2},{4,5},{5,4},{6,7},{7,6},{8,9},{9,8},{10,11... | collective-permute-start | bytes 2359304 | tf_op jit(solution)/shard_map/ppermute | solution.py:52
  3.3 0.9 %copy-start.1 = (bf16[2,6,128,256]{3,2,1,0:T(8,128)(2,1)}, bf16[2,6,128,256]{3,2,1,0:T(8,128)(2,1)S(1)}, u32[]{:S(2)}) copy-start(bf16[2,6,128,256]{3,2,1,0:T(8,128)(2,1)S(1)} %collective-permute-done.pair) | copy-start | bytes 2359300
  5.8 24.8 %collective-permute-start.5 = (bf16[256,768]{1,0:T(8,128)(2,1)S(1)}, bf16[256,768]{1,0:T(8,128)(2,1)S(1)}, u32[]{:S(2)}, u32[]{:S(2)}) collective-permute-start(bf16[256,768]{1,0:T(8,128)(2,1)S(1)} %get-tuple-element.39), channel_id=1, source_target_pairs={{0,14},{1,15},{2,0},{3,1},{4,2},{5,3},{6,4},{7,5},{8,6},{9,7},{10,... | collective-permute-start | bytes 1179656 | tf_op jit(solution)/shard_map/ppermute | solution.py:47
  12.7 1.3 %collective-permute-start.1 = (f32[54,2,128]{2,1,0:T(2,128)S(1)}, f32[54,2,128]{2,1,0:T(2,128)S(1)}, u32[]{:S(2)}, u32[]{:S(2)}) collective-permute-start(f32[54,2,128]{2,1,0:T(2,128)S(1)} %get-tuple-element.28), channel_id=1, source_target_pairs={{0,1},{1,0},{2,3},{3,2},{4,5},{5,4},{6,7},{7,6},{8,9},{9,8},{10,11... | collective-permute-start | bytes 165896 | tf_op jit(solution)/shard_map/ppermute | solution.py:52
  14.2 8.8 %collective-permute-start.2 = (bf16[54,6,128]{2,1,0:T(8,128)(2,1)S(1)}, bf16[54,6,128]{2,1,0:T(8,128)(2,1)S(1)}, u32[]{:S(2)}, u32[]{:S(2)}) collective-permute-start(bf16[54,6,128]{2,1,0:T(8,128)(2,1)S(1)} %get-tuple-element.29), channel_id=1, source_target_pairs={{0,2},{1,3},{2,4},{3,5},{4,6},{5,7},{6,8},{7,9},{8,10},{9,11},{10,... | collective-permute-start | bytes 248840 | tf_op jit(solution)/shard_map/ppermute | solution.py:47
  14.3 8.8 %collective-permute-start.3 = (bf16[54,6,128]{2,1,0:T(8,128)(2,1)S(1)}, bf16[54,6,128]{2,1,0:T(8,128)(2,1)S(1)}, u32[]{:S(2)}, u32[]{:S(2)}) collective-permute-start(bf16[54,6,128]{2,1,0:T(8,128)(2,1)S(1)} %get-tuple-element.31), channel_id=1, source_target_pairs={{0,14},{1,15},{2,0},{3,1},{4,2},{5,3},{6,4},{7,5},{8,6},{9,7},{10,... | collective-permute-start | bytes 248840 | tf_op jit(solution)/shard_map/ppermute | solution.py:47
  28.0 6.3 %collective-permute-start.4 = (f32[2,128,128]{2,1,0:T(8,128)S(1)}, f32[2,128,128]{2,1,0:T(8,128)S(1)}, u32[]{:S(2)}, u32[]{:S(2)}) collective-permute-start(f32[2,128,128]{2,1,0:T(8,128)S(1)} %get-tuple-element.38), channel_id=1, source_target_pairs={{0,2},{1,3},{2,0},{3,1},{4,6},{5,7},{6,4},{7,5},{8,10},{9,11},{10,... | collective-permute-start | bytes 393224 | tf_op jit(solution)/shard_map/ppermute | solution.py:52
  32.5 4.3 %collective-permute-start.6 = (bf16[2,128,128]{2,1,0:T(8,128)(2,1)S(1)}, bf16[2,128,128]{2,1,0:T(8,128)(2,1)S(1)}, u32[]{:S(2)}, u32[]{:S(2)}) collective-permute-start(bf16[2,128,128]{2,1,0:T(8,128)(2,1)S(1)} %get-tuple-element.41), channel_id=1, source_target_pairs={{0,2},{1,3},{2,0},{3,1},{4,6},{5,7},{6,4},{7,5},{8,10},{9,11},{10,... | collective-permute-start | bytes 196616 | tf_op jit(solution)/shard_map/ppermute | solution.py:52
  36.9 5.0 %collective-permute-start.7 = (f32[2,128,128]{2,1,0:T(8,128)S(1)}, f32[2,128,128]{2,1,0:T(8,128)S(1)}, u32[]{:S(2)}, u32[]{:S(2)}) collective-permute-start(f32[2,128,128]{2,1,0:T(8,128)S(1)} %get-tuple-element.43), channel_id=1, source_target_pairs={{0,4},{1,5},{2,6},{3,7},{4,0},{5,1},{6,2},{7,3},{8,12},{9,13},{10,... | collective-permute-start | bytes 393224 | tf_op jit(solution)/shard_map/ppermute | solution.py:52
  41.9 7.7 %copy-start = (bf16[2,2,2,128,128]{4,3,2,1,0:T(8,128)(2,1)S(1)}, bf16[2,2,2,128,128]{4,3,2,1,0:T(8,128)(2,1)}, u32[]{:S(2)}) copy-start(bf16[2,2,2,128,128]{4,3,2,1,0:T(8,128)(2,1)} %tau.1) | copy-start | bytes 786436
  42.0 6.3 %collective-permute-start.8 = (bf16[2,128,128]{2,1,0:T(8,128)(2,1)S(1)}, bf16[2,128,128]{2,1,0:T(8,128)(2,1)S(1)}, u32[]{:S(2)}, u32[]{:S(2)}) collective-permute-start(bf16[2,128,128]{2,1,0:T(8,128)(2,1)S(1)} %shard_map.85.mine), channel_id=1, source_target_pairs={{0,8},{1,9},{2,10},{3,11},{4,12},{5,13},{6,14},{7,15},{8,0},{9,1},... | collective-permute-start | bytes 196616 | tf_op jit(solution)/shard_map/ppermute | solution.py:52
  48.2 1.4 %collective-permute-start.9 = (f32[2,128,128]{2,1,0:T(8,128)S(1)}, f32[2,128,128]{2,1,0:T(8,128)S(1)}, u32[]{:S(2)}, u32[]{:S(2)}) collective-permute-start(f32[2,128,128]{2,1,0:T(8,128)S(1)} %shard_map.86.mine), channel_id=1, source_target_pairs={{0,1},{1,0},{2,3},{3,2},{4,5},{5,4},{6,7},{7,6},{8,9},{9,8},{10,11... | collective-permute-start | bytes 393224 | tf_op jit(solution)/shard_map/ppermute | solution.py:52
  50.2 3.8 %collective-permute-start.10 = (f32[40,128]{1,0:T(8,128)S(1)}, f32[40,128]{1,0:T(8,128)S(1)}, u32[]{:S(2)}, u32[]{:S(2)}) collective-permute-start(f32[40,128]{1,0:T(8,128)S(1)} %get-tuple-element.45), channel_id=1, source_target_pairs={{0,2},{1,3},{2,0},{3,1},{4,6},{5,7},{6,4},{7,5},{8,10},{9,11},{10,... | collective-permute-start | bytes 61448 | tf_op jit(solution)/shard_map/ppermute | solution.py:52
  50.9 3.8 %collective-permute-start.11 = (f32[40,128]{1,0:T(8,128)S(1)}, f32[40,128]{1,0:T(8,128)S(1)}, u32[]{:S(2)}, u32[]{:S(2)}) collective-permute-start(f32[40,128]{1,0:T(8,128)S(1)} %get-tuple-element.46), channel_id=1, source_target_pairs={{0,4},{1,5},{2,6},{3,7},{4,0},{5,1},{6,2},{7,3},{8,12},{9,13},{10,... | collective-permute-start | bytes 61448 | tf_op jit(solution)/shard_map/ppermute | solution.py:52
  52.8 4.7 %collective-permute-start.12 = (f32[40,128]{1,0:T(8,128)S(1)}, f32[40,128]{1,0:T(8,128)S(1)}, u32[]{:S(2)}, u32[]{:S(2)}) collective-permute-start(f32[40,128]{1,0:T(8,128)S(1)} %get-tuple-element.47), channel_id=1, source_target_pairs={{0,6},{1,7},{2,4},{3,5},{4,2},{5,3},{6,0},{7,1},{8,14},{9,15},{10,... | collective-permute-start | bytes 61448 | tf_op jit(solution)/shard_map/ppermute | solution.py:52
where the time goes:
time: 58.3 us; the launch traced here: 58.2 us
  starting transfers between devices  23.3 us (40%)
  waiting for transfers between devices  22.4 us (38%)
  Pallas kernels  10.9 us (19%)
  local copies, waits for them, and re-layouts  0.89 us (2%)
  between operations  0.73 us (1%)
    ppermute x10, waiting for transfers between devices, swapped(): return lax.ppermute(value, 'space', [(i, i ^ bit) for i in range(size)])  18.3 us
    ppermute x10, starting transfers between devices, swapped(): return lax.ppermute(value, 'space', [(i, i ^ bit) for i in range(size)])  12.5 us
    pallas_call x12, Pallas kernels, call(): return run(*ins)  10.9 us
    ppermute x3, starting transfers between devices, shifted(): lax.ppermute(value, 'space', [(i, (i + by) % size) for i in range(size)])  10.7 us
    ppermute x3, waiting for transfers between devices, shifted(): lax.ppermute(value, 'space', [(i, (i + by) % size) for i in range(size)])  4.07 us
  transfers between devices with their start and end apart: 13, of which 11 were waited for; matrix products, arithmetic and copies ran while one was open for 0% of the time, Pallas kernels for 14%

commit v1 on v0

--- a/solution.py
+++ b/solution.py
@@ -379,18 +379,22 @@
     phase[1] = -jnp.where(turn >= 2, -small, small)
 
 
-def elemental_kernel(scale, ops, pos, links, phase, ordered, *refs):
-    nears, (send, keep, right) = refs[:-3], refs[-3:]
-    planes, rows, width = ordered.shape
+def elemental_kernel(scale, ops, planes, stage, pos, links, phase, ordered, *refs):
+    count_outs = 2 if stage == "part" else 3
+    nears, outs = refs[:-count_outs], refs[-count_outs:]
+    right = outs[-1]
+    if stage == "rest":
+        before, nears = nears[0], nears[1:]
+    rows, width = ordered.shape[1:]
     count, sites = rows // 2, width // 3
     up = (pos[0] >> 1) & 1
     sub = 16
     grams = []
     for at, k in enumerate(ops):
         m = k % 3
-        near = nears[at % len(nears)] if m else None
-        gram = None
-        for p in range(planes):
+        near = nears[at] if m else None
+        gram = before[at] if stage == "rest" else None
+        for p in planes:
             for h in range(2):
                 pr, pi = (phase[r, 4 * k + 2 * p + h : 4 * k + 2 * p + h + 1, :] for r in range(2))
                 coef = []
@@ -409,7 +413,7 @@
                             at_rows = slice(r * count + i * sub, r * count + (i + 1) * sub)
                             if m:
                                 got = near[p, at_rows, cols]
-                            elif p + 1 < planes:
+                            elif p == 0:
                                 got = ordered[p + 1, at_rows, cols]
                             else:
                                 got = nears[0][at_rows, cols]
@@ -425,12 +429,18 @@
                 ordered[p], right[at, p], (((1,), (1,)), ((), ())), preferred_element_type=F32
             )
             gram = part if gram is None else gram + part
+        if stage == "part":
+            outs[0][at] = gram
+            continue
         grams.append(
             (
                 (gram[:count, :count] + gram[count:, count:]) * scale,
                 (gram[:count, count:] - gram[count:, :count]) * scale,
             )
         )
+    if stage == "part":
+        return
+    send, keep = outs[:2]
     for r in range(2):
         first, second = grams[0][r], grams[1][r]
         send[r] = jnp.where(up == 1, first, second).astype(send.dtype)
@@ -571,21 +581,22 @@
     )
     flat = (2, count, count)
 
-    def grams(ops, nears, kind):
+    def grams(ops, planes, stage, nears, outs):
         return call(
-            lambda *refs: elemental_kernel(scale, ops, *refs),
-            [(flat, kind), (flat, F32)],
+            lambda *refs: elemental_kernel(scale, ops, planes, stage, *refs),
+            outs,
             [pos, smeared, phase, ordered] + nears,
             scalars=1,
             scratch=[pltpu.VMEM((2,) + wide, BF16)],
         )
 
-    send, early = grams((1, 2), [near_y, near_z], F32)
+    send, early = grams((1, 2), (0, 1), "all", [near_y, near_z], [(flat, F32), (flat, F32)])
     early_in = swapped(send, 2)
-    send, late = grams((0, 3), [near_x], BF16)
+    (part,) = grams((0, 3), (0,), "part", [], [((2, 2 * count, 2 * count), F32)])
+    send, late = grams((0, 3), (1,), "rest", [part, near_x], [(flat, BF16), (flat, F32)])
     late_in = swapped(send, 2)
     send, keep = call(
-        split_kernel, [(flat, F32), (flat, F32)], [pos, early, early_in, late, late_in], scalars=1
+        split_kernel, [(flat, BF16), (flat, F32)], [pos, early, early_in, late, late_in], scalars=1
     )
     bit = 8
     other = swapped(send, 4)

time: 58.3 us -> 57.6 us (0.988)
  waiting for transfers between devices: 22.4 us -> 21.5 us
    ppermute x10, waiting for transfers between devices: 18.3 us -> 17.4 us  [swapped(): return lax.ppermute(value, 'space', [(i, i ^ bit) for i in range(size)])]
    pallas_call x12 -> x13, Pallas kernels: 10.9 us -> 11.1 us  [call(): return run(*ins)]
where the time goes in v1:
time: 57.6 us; the launch traced here: 57.5 us
  starting transfers between devices  23.3 us (40%)
  waiting for transfers between devices  21.5 us (37%)
  Pallas kernels  11.1 us (19%)
  local copies, waits for them, and re-layouts  0.89 us (2%)
  between operations  0.74 us (1%)
    ppermute x10, waiting for transfers between devices, swapped(): return lax.ppermute(value, 'space', [(i, i ^ bit) for i in range(size)])  17.4 us
    ppermute x10, starting transfers between devices, swapped(): return lax.ppermute(value, 'space', [(i, i ^ bit) for i in range(size)])  12.5 us
    pallas_call x13, Pallas kernels, call(): return run(*ins)  11.1 us
    ppermute x3, starting transfers between devices, shifted(): lax.ppermute(value, 'space', [(i, (i + by) % size) for i in range(size)])  10.7 us
    ppermute x3, waiting for transfers between devices, shifted(): lax.ppermute(value, 'space', [(i, (i + by) % size) for i in range(size)])  4.07 us
  transfers between devices with their start and end apart: 13, of which 11 were waited for; matrix products, arithmetic and copies ran while one was open for 0% of the time, Pallas kernels for 14%

profile of v1, /device:TPU:0, one launch (start us, length us, event | category | flops | bytes accessed | tf_op | source)
XLA Modules:
  0.0 57.5 jit_solution(2222373547251841781)
XLA Ops:
  0.6 0.6 collective-permute-start
  1.2 2.1 %collective-permute-done.pair = bf16[2,6,128,256]{3,2,1,0:T(8,128)(2,1)S(1)} collective-permute-done((bf16[2,6,128,256]{3,2,1,0:T(8,128)(2,1)}, bf16[2,6,128,256]{3,2,1,0:T(8,128)(2,1)S(1)}, u32[]{:S(2)}, u32[]{:S(2)}) %collective-permute-start) | collective-permute-done | bytes 786464 | tf_op jit(solution)/shard_map/ppermute | solution.py:52
  3.3 0.0 copy-start.1
  3.3 0.9 %copy-done.1 = bf16[2,6,128,256]{3,2,1,0:T(8,128)(2,1)} copy-done((bf16[2,6,128,256]{3,2,1,0:T(8,128)(2,1)}, bf16[2,6,128,256]{3,2,1,0:T(8,128)(2,1)S(1)}, u32[]{:S(2)}) %copy-start.1) | copy-done | bytes 786456
  4.2 1.6 %shard_map.77 = (bf16[2,256,768]{2,1,0:T(8,128)(2,1)S(1)}, bf16[256,768]{1,0:T(8,128)(2,1)S(1)}, s32[4,3]{1,0:T(4,128)S(1)}, s32[1,8]{1,0:T(1,128)S(1)}) custom-call(s32[1]{0:T(128)} %bitcast.pos.refs_0_, bf16[2,6,128,256]{3,2,1,0:T(8,128)(2,1)} %bitcast.14, bf16[2,6,128,256]{3,2,1,0:T(8,128)(2,1)} %copy-done.1, s32[2,128]{1,0:T(2,128)} %order.1, ...), custom_call_target="tpu_custom_call" | custom-call | flops 1000000 | bytes 1000000 | tf_op jit(solution)/shard_map/pallas_call | solution.py:42
  5.8 6.0 %collective-permute-start.5 = (bf16[256,768]{1,0:T(8,128)(2,1)S(1)}, bf16[256,768]{1,0:T(8,128)(2,1)S(1)}, u32[]{:S(2)}, u32[]{:S(2)}) collective-permute-start(bf16[256,768]{1,0:T(8,128)(2,1)S(1)} %get-tuple-element.39), channel_id=1, source_target_pairs={{0,14},{1,15},{2,0},{3,1},{4,2},{5,3},{6,4},{7,5},{8,6},{9,7},{10,... | collective-permute-start | bytes 1179656 | tf_op jit(solution)/shard_map/ppermute | solution.py:47
  11.7 0.9 %shard_map.78 = (f32[54,2,128]{2,1,0:T(2,128)S(1)}, f32[54,2,128]{2,1,0:T(2,128)S(1)}) custom-call(s32[1]{0:T(128)} %bitcast.pos.refs_0_, f32[54,4,128]{2,1,0:T(4,128)} %bitcast.15), custom_call_target="tpu_custom_call" | custom-call | flops 1000000 | bytes 1000000 | tf_op jit(solution)/shard_map/pallas_call | solution.py:42
  12.7 0.1 collective-permute-start.1
  12.8 1.2 %collective-permute-done.1.links_in = f32[54,2,128]{2,1,0:T(2,128)S(1)} collective-permute-done((f32[54,2,128]{2,1,0:T(2,128)S(1)}, f32[54,2,128]{2,1,0:T(2,128)S(1)}, u32[]{:S(2)}, u32[]{:S(2)}) %collective-permute-start.1) | collective-permute-done | bytes 55328 | tf_op jit(solution)/shard_map/ppermute | solution.py:52
  14.0 0.2 shard_map.79
  14.2 0.1 collective-permute-start.2
  14.3 4.7 %collective-permute-start.3 = (bf16[54,6,128]{2,1,0:T(8,128)(2,1)S(1)}, bf16[54,6,128]{2,1,0:T(8,128)(2,1)S(1)}, u32[]{:S(2)}, u32[]{:S(2)}) collective-permute-start(bf16[54,6,128]{2,1,0:T(8,128)(2,1)S(1)} %get-tuple-element.31), channel_id=1, source_target_pairs={{0,14},{1,15},{2,0},{3,1},{4,2},{5,3},{6,4},{7,5},{8,6},{9,7},{10,... | collective-permute-start | bytes 248840 | tf_op jit(solution)/shard_map/ppermute | solution.py:47
  19.0 4.1 %collective-permute-done.2.below = bf16[54,6,128]{2,1,0:T(8,128)(2,1)S(1)} collective-permute-done((bf16[54,6,128]{2,1,0:T(8,128)(2,1)S(1)}, bf16[54,6,128]{2,1,0:T(8,128)(2,1)S(1)}, u32[]{:S(2)}, u32[]{:S(2)}) %collective-permute-start.2) | collective-permute-done | bytes 82976 | tf_op jit(solution)/shard_map/ppermute | solution.py:47
  23.0 0.0 collective-permute-done.3.above
  23.0 2.3 %shard_map.80.refs_1_ = f32[54,4,128]{2,1,0:T(4,128)S(1)} custom-call(bf16[54,6,128]{2,1,0:T(8,128)(2,1)S(1)} %collective-permute-done.2.below, f32[54,4,128]{2,1,0:T(4,128)S(1)} %get-tuple-element.30.own, bf16[54,6,128]{2,1,0:T(8,128)(2,1)S(1)} %collective-permute-done.3.above), custom_call_target="tpu_custom_call" | custom-call | flops 1000000 | bytes 1000000 | tf_op jit(solution)/shard_map/pallas_call | solution.py:42
  25.4 0.6 %shard_map.81 = (bf16[2,256,768]{2,1,0:T(8,128)(2,1)S(1)}, bf16[2,256,768]{2,1,0:T(8,128)(2,1)S(1)}, f32[2,16,128]{2,1,0:T(8,128)S(1)}) custom-call(s32[1]{0:T(128)} %bitcast.pos.refs_0_, s32[4,3]{1,0:T(4,128)S(1)} %get-tuple-element.32.refs_1_, bf16[2,256,768]{2,1,0:T(8,128)(2,1)S(1)} %get-tuple-element.33.refs_2_.refs_3_), custom_call_target="tpu_custom_call" | custom-call | flops 1000000 | bytes 1000000 | tf_op jit(solution)/shard_map/pallas_call | solution.py:42
  26.0 2.0 %shard_map.82 = (f32[2,128,128]{2,1,0:T(8,128)S(1)}, f32[2,128,128]{2,1,0:T(8,128)S(1)}) custom-call(s32[1]{0:T(128)} %bitcast.pos.refs_0_, f32[54,4,128]{2,1,0:T(4,128)S(1)} %shard_map.80.refs_1_, f32[2,16,128]{2,1,0:T(8,128)S(1)} %get-tuple-element.34.refs_2_, bf16[2,256,768]{2,1,0:T(8,128)(2,1)S(1)} %get-tuple-element.33.refs_2_.refs_3_, ...), custom_call_target="tpu_custom_call" | custom-call | flops 1000000 | bytes 1000000 | tf_op jit(solution)/shard_map/pallas_call | solution.py:42
  28.0 2.5 %collective-permute-start.4 = (f32[2,128,128]{2,1,0:T(8,128)S(1)}, f32[2,128,128]{2,1,0:T(8,128)S(1)}, u32[]{:S(2)}, u32[]{:S(2)}) collective-permute-start(f32[2,128,128]{2,1,0:T(8,128)S(1)} %get-tuple-element.38), channel_id=1, source_target_pairs={{0,2},{1,3},{2,0},{3,1},{4,6},{5,7},{6,4},{7,5},{8,10},{9,11},{10,... | collective-permute-start | bytes 393224 | tf_op jit(solution)/shard_map/ppermute | solution.py:52
  30.6 1.1 %shard_map.83.refs_4_ = f32[2,256,256]{2,1,0:T(8,128)S(1)} custom-call(s32[1]{0:T(128)} %bitcast.pos.refs_0_, f32[54,4,128]{2,1,0:T(4,128)S(1)} %shard_map.80.refs_1_, f32[2,16,128]{2,1,0:T(8,128)S(1)} %get-tuple-element.34.refs_2_, bf16[2,256,768]{2,1,0:T(8,128)(2,1)S(1)} %get-tuple-element.33.refs_2_.refs_3_), custom_call_target="tpu_custom_call" | custom-call | flops 1000000 | bytes 1000000 | tf_op jit(solution)/shard_map/pallas_call | solution.py:42
  31.6 0.0 collective-permute-done.5.refs_5_
  31.7 1.1 %shard_map.84 = (bf16[2,128,128]{2,1,0:T(8,128)(2,1)S(1)}, f32[2,128,128]{2,1,0:T(8,128)S(1)}) custom-call(s32[1]{0:T(128)} %bitcast.pos.refs_0_, f32[54,4,128]{2,1,0:T(4,128)S(1)} %shard_map.80.refs_1_, f32[2,16,128]{2,1,0:T(8,128)S(1)} %get-tuple-element.34.refs_2_, bf16[2,256,768]{2,1,0:T(8,128)(2,1)S(1)} %get-tuple-element.33.refs_2_.refs_3_, ...), custom_call_target="tpu_custom_call" | custom-call | flops 1000000 | bytes 1000000 | tf_op jit(solution)/shard_map/pallas_call | solution.py:42
  32.8 0.1 collective-permute-start.6
  32.8 1.4 %collective-permute-done.4.early_in = f32[2,128,128]{2,1,0:T(8,128)S(1)} collective-permute-done((f32[2,128,128]{2,1,0:T(8,128)S(1)}, f32[2,128,128]{2,1,0:T(8,128)S(1)}, u32[]{:S(2)}, u32[]{:S(2)}) %collective-permute-start.4) | collective-permute-done | bytes 131104 | tf_op jit(solution)/shard_map/ppermute | solution.py:52
  34.3 2.8 %collective-permute-done.6.late_in = bf16[2,128,128]{2,1,0:T(8,128)(2,1)S(1)} collective-permute-done((bf16[2,128,128]{2,1,0:T(8,128)(2,1)S(1)}, bf16[2,128,128]{2,1,0:T(8,128)(2,1)S(1)}, u32[]{:S(2)}, u32[]{:S(2)}) %collective-permute-start.6) | collective-permute-done | bytes 65568 | tf_op jit(solution)/shard_map/ppermute | solution.py:52
  37.1 1.6 %collective-permute-start.7 = (bf16[2,128,128]{2,1,0:T(8,128)(2,1)S(1)}, bf16[2,128,128]{2,1,0:T(8,128)(2,1)S(1)}, u32[]{:S(2)}, u32[]{:S(2)}) collective-permute-start(bf16[2,128,128]{2,1,0:T(8,128)(2,1)S(1)} %get-tuple-element.43), channel_id=1, source_target_pairs={{0,4},{1,5},{2,6},{3,7},{4,0},{5,1},{6,2},{7,3},{8,12},{9,13},{10,... | collective-permute-start | bytes 196616 | tf_op jit(solution)/shard_map/ppermute | solution.py:52
  38.8 2.7 %collective-permute-done.7.other = bf16[2,128,128]{2,1,0:T(8,128)(2,1)S(1)} collective-permute-done((bf16[2,128,128]{2,1,0:T(8,128)(2,1)S(1)}, bf16[2,128,128]{2,1,0:T(8,128)(2,1)S(1)}, u32[]{:S(2)}, u32[]{:S(2)}) %collective-permute-start.7) | collective-permute-done | bytes 65568 | tf_op jit(solution)/shard_map/ppermute | solution.py:52
  41.5 0.0 copy-start
  41.5 4.0 %collective-permute-start.8 = (bf16[2,128,128]{2,1,0:T(8,128)(2,1)S(1)}, bf16[2,128,128]{2,1,0:T(8,128)(2,1)S(1)}, u32[]{:S(2)}, u32[]{:S(2)}) collective-permute-start(bf16[2,128,128]{2,1,0:T(8,128)(2,1)S(1)} %shard_map.86.mine), channel_id=1, source_target_pairs={{0,8},{1,9},{2,10},{3,11},{4,12},{5,13},{6,14},{7,15},{8,0},{9,1},... | collective-permute-start | bytes 196616 | tf_op jit(solution)/shard_map/ppermute | solution.py:52
  45.5 2.2 %collective-permute-done.8.other = bf16[2,128,128]{2,1,0:T(8,128)(2,1)S(1)} collective-permute-done((bf16[2,128,128]{2,1,0:T(8,128)(2,1)S(1)}, bf16[2,128,128]{2,1,0:T(8,128)(2,1)S(1)}, u32[]{:S(2)}, u32[]{:S(2)}) %collective-permute-start.8) | collective-permute-done | bytes 65568 | tf_op jit(solution)/shard_map/ppermute | solution.py:52
  47.8 0.1 collective-permute-start.9
  47.8 1.3 %collective-permute-done.9.other = f32[2,128,128]{2,1,0:T(8,128)S(1)} collective-permute-done((f32[2,128,128]{2,1,0:T(8,128)S(1)}, f32[2,128,128]{2,1,0:T(8,128)S(1)}, u32[]{:S(2)}, u32[]{:S(2)}) %collective-permute-start.9) | collective-permute-done | bytes 131104 | tf_op jit(solution)/shard_map/ppermute | solution.py:52
  49.2 0.0 copy-done
  49.2 0.5 shard_map.88
  49.7 0.4 collective-permute-start.10
  50.1 2.0 %collective-permute-start.11 = (f32[40,128]{1,0:T(8,128)S(1)}, f32[40,128]{1,0:T(8,128)S(1)}, u32[]{:S(2)}, u32[]{:S(2)}) collective-permute-start(f32[40,128]{1,0:T(8,128)S(1)} %get-tuple-element.46), channel_id=1, source_target_pairs={{0,4},{1,5},{2,6},{3,7},{4,0},{5,1},{6,2},{7,3},{8,12},{9,13},{10,... | collective-permute-start | bytes 61448 | tf_op jit(solution)/shard_map/ppermute | solution.py:52
  52.1 1.2 %collective-permute-start.12 = (f32[40,128]{1,0:T(8,128)S(1)}, f32[40,128]{1,0:T(8,128)S(1)}, u32[]{:S(2)}, u32[]{:S(2)}) collective-permute-start(f32[40,128]{1,0:T(8,128)S(1)} %get-tuple-element.47), channel_id=1, source_target_pairs={{0,6},{1,7},{2,4},{3,5},{4,2},{5,3},{6,0},{7,1},{8,14},{9,15},{10,... | collective-permute-start | bytes 61448 | tf_op jit(solution)/shard_map/ppermute | solution.py:52
  53.3 0.3 collective-permute-done.10.refs_3_
  53.6 0.3 collective-permute-done.11.refs_4_
  53.9 2.9 %collective-permute-done.12.refs_5_ = f32[40,128]{1,0:T(8,128)S(1)} collective-permute-done((f32[40,128]{1,0:T(8,128)S(1)}, f32[40,128]{1,0:T(8,128)S(1)}, u32[]{:S(2)}, u32[]{:S(2)}) %collective-permute-start.12) | collective-permute-done | bytes 20512 | tf_op jit(solution)/shard_map/ppermute | solution.py:52
  56.8 0.7 %shard_map.89 = (f32[4,32,128]{2,1,0:T(8,128)}, f32[4,2,8]{2,1,0:T(2,128)}) custom-call(s32[1]{0:T(128)} %bitcast.pos.refs_0_, s32[1,8]{1,0:T(1,128)S(1)} %get-tuple-element.26.refs_1_, f32[40,128]{1,0:T(8,128)S(1)} %get-tuple-element.44.refs_2_, f32[40,128]{1,0:T(8,128)S(1)} %collective-permute-done.10.refs_3_, ...), custom_call_target="tpu_custom_call" | custom-call | flops 1000000 | bytes 1000000 | tf_op jit(solution)/shard_map/pallas_call | solution.py:42
  (3 shorter events, 0.1 us)
Async XLA Ops:
  0.6 2.7 %collective-permute-start = (bf16[2,6,128,256]{3,2,1,0:T(8,128)(2,1)}, bf16[2,6,128,256]{3,2,1,0:T(8,128)(2,1)S(1)}, u32[]{:S(2)}, u32[]{:S(2)}) collective-permute-start(bf16[2,6,128,256]{3,2,1,0:T(8,128)(2,1)} %bitcast.13), channel_id=1, source_target_pairs={{0,1},{1,0},{2,3},{3,2},{4,5},{5,4},{6,7},{7,6},{8,9},{9,8},{10,11... | collective-permute-start | bytes 2359304 | tf_op jit(solution)/shard_map/ppermute | solution.py:52
  3.3 0.9 %copy-start.1 = (bf16[2,6,128,256]{3,2,1,0:T(8,128)(2,1)}, bf16[2,6,128,256]{3,2,1,0:T(8,128)(2,1)S(1)}, u32[]{:S(2)}) copy-start(bf16[2,6,128,256]{3,2,1,0:T(8,128)(2,1)S(1)} %collective-permute-done.pair) | copy-start | bytes 2359300
  5.8 25.9 %collective-permute-start.5 = (bf16[256,768]{1,0:T(8,128)(2,1)S(1)}, bf16[256,768]{1,0:T(8,128)(2,1)S(1)}, u32[]{:S(2)}, u32[]{:S(2)}) collective-permute-start(bf16[256,768]{1,0:T(8,128)(2,1)S(1)} %get-tuple-element.39), channel_id=1, source_target_pairs={{0,14},{1,15},{2,0},{3,1},{4,2},{5,3},{6,4},{7,5},{8,6},{9,7},{10,... | collective-permute-start | bytes 1179656 | tf_op jit(solution)/shard_map/ppermute | solution.py:47
  12.7 1.3 %collective-permute-start.1 = (f32[54,2,128]{2,1,0:T(2,128)S(1)}, f32[54,2,128]{2,1,0:T(2,128)S(1)}, u32[]{:S(2)}, u32[]{:S(2)}) collective-permute-start(f32[54,2,128]{2,1,0:T(2,128)S(1)} %get-tuple-element.28), channel_id=1, source_target_pairs={{0,1},{1,0},{2,3},{3,2},{4,5},{5,4},{6,7},{7,6},{8,9},{9,8},{10,11... | collective-permute-start | bytes 165896 | tf_op jit(solution)/shard_map/ppermute | solution.py:52
  14.2 8.8 %collective-permute-start.2 = (bf16[54,6,128]{2,1,0:T(8,128)(2,1)S(1)}, bf16[54,6,128]{2,1,0:T(8,128)(2,1)S(1)}, u32[]{:S(2)}, u32[]{:S(2)}) collective-permute-start(bf16[54,6,128]{2,1,0:T(8,128)(2,1)S(1)} %get-tuple-element.29), channel_id=1, source_target_pairs={{0,2},{1,3},{2,4},{3,5},{4,6},{5,7},{6,8},{7,9},{8,10},{9,11},{10,... | collective-permute-start | bytes 248840 | tf_op jit(solution)/shard_map/ppermute | solution.py:47
  14.3 8.8 %collective-permute-start.3 = (bf16[54,6,128]{2,1,0:T(8,128)(2,1)S(1)}, bf16[54,6,128]{2,1,0:T(8,128)(2,1)S(1)}, u32[]{:S(2)}, u32[]{:S(2)}) collective-permute-start(bf16[54,6,128]{2,1,0:T(8,128)(2,1)S(1)} %get-tuple-element.31), channel_id=1, source_target_pairs={{0,14},{1,15},{2,0},{3,1},{4,2},{5,3},{6,4},{7,5},{8,6},{9,7},{10,... | collective-permute-start | bytes 248840 | tf_op jit(solution)/shard_map/ppermute | solution.py:47
  28.0 6.3 %collective-permute-start.4 = (f32[2,128,128]{2,1,0:T(8,128)S(1)}, f32[2,128,128]{2,1,0:T(8,128)S(1)}, u32[]{:S(2)}, u32[]{:S(2)}) collective-permute-start(f32[2,128,128]{2,1,0:T(8,128)S(1)} %get-tuple-element.38), channel_id=1, source_target_pairs={{0,2},{1,3},{2,0},{3,1},{4,6},{5,7},{6,4},{7,5},{8,10},{9,11},{10,... | collective-permute-start | bytes 393224 | tf_op jit(solution)/shard_map/ppermute | solution.py:52
  32.8 4.3 %collective-permute-start.6 = (bf16[2,128,128]{2,1,0:T(8,128)(2,1)S(1)}, bf16[2,128,128]{2,1,0:T(8,128)(2,1)S(1)}, u32[]{:S(2)}, u32[]{:S(2)}) collective-permute-start(bf16[2,128,128]{2,1,0:T(8,128)(2,1)S(1)} %get-tuple-element.41), channel_id=1, source_target_pairs={{0,2},{1,3},{2,0},{3,1},{4,6},{5,7},{6,4},{7,5},{8,10},{9,11},{10,... | collective-permute-start | bytes 196616 | tf_op jit(solution)/shard_map/ppermute | solution.py:52
  37.1 4.3 %collective-permute-start.7 = (bf16[2,128,128]{2,1,0:T(8,128)(2,1)S(1)}, bf16[2,128,128]{2,1,0:T(8,128)(2,1)S(1)}, u32[]{:S(2)}, u32[]{:S(2)}) collective-permute-start(bf16[2,128,128]{2,1,0:T(8,128)(2,1)S(1)} %get-tuple-element.43), channel_id=1, source_target_pairs={{0,4},{1,5},{2,6},{3,7},{4,0},{5,1},{6,2},{7,3},{8,12},{9,13},{10,... | collective-permute-start | bytes 196616 | tf_op jit(solution)/shard_map/ppermute | solution.py:52
  41.5 7.7 %copy-start = (bf16[2,2,2,128,128]{4,3,2,1,0:T(8,128)(2,1)S(1)}, bf16[2,2,2,128,128]{4,3,2,1,0:T(8,128)(2,1)}, u32[]{:S(2)}) copy-start(bf16[2,2,2,128,128]{4,3,2,1,0:T(8,128)(2,1)} %tau.1) | copy-start | bytes 786436
  41.5 6.3 %collective-permute-start.8 = (bf16[2,128,128]{2,1,0:T(8,128)(2,1)S(1)}, bf16[2,128,128]{2,1,0:T(8,128)(2,1)S(1)}, u32[]{:S(2)}, u32[]{:S(2)}) collective-permute-start(bf16[2,128,128]{2,1,0:T(8,128)(2,1)S(1)} %shard_map.86.mine), channel_id=1, source_target_pairs={{0,8},{1,9},{2,10},{3,11},{4,12},{5,13},{6,14},{7,15},{8,0},{9,1},... | collective-permute-start | bytes 196616 | tf_op jit(solution)/shard_map/ppermute | solution.py:52
  47.8 1.4 %collective-permute-start.9 = (f32[2,128,128]{2,1,0:T(8,128)S(1)}, f32[2,128,128]{2,1,0:T(8,128)S(1)}, u32[]{:S(2)}, u32[]{:S(2)}) collective-permute-start(f32[2,128,128]{2,1,0:T(8,128)S(1)} %shard_map.87.mine), channel_id=1, source_target_pairs={{0,1},{1,0},{2,3},{3,2},{4,5},{5,4},{6,7},{7,6},{8,9},{9,8},{10,11... | collective-permute-start | bytes 393224 | tf_op jit(solution)/shard_map/ppermute | solution.py:52
  49.7 3.8 %collective-permute-start.10 = (f32[40,128]{1,0:T(8,128)S(1)}, f32[40,128]{1,0:T(8,128)S(1)}, u32[]{:S(2)}, u32[]{:S(2)}) collective-permute-start(f32[40,128]{1,0:T(8,128)S(1)} %get-tuple-element.45), channel_id=1, source_target_pairs={{0,2},{1,3},{2,0},{3,1},{4,6},{5,7},{6,4},{7,5},{8,10},{9,11},{10,... | collective-permute-start | bytes 61448 | tf_op jit(solution)/shard_map/ppermute | solution.py:52
  50.1 3.8 %collective-permute-start.11 = (f32[40,128]{1,0:T(8,128)S(1)}, f32[40,128]{1,0:T(8,128)S(1)}, u32[]{:S(2)}, u32[]{:S(2)}) collective-permute-start(f32[40,128]{1,0:T(8,128)S(1)} %get-tuple-element.46), channel_id=1, source_target_pairs={{0,4},{1,5},{2,6},{3,7},{4,0},{5,1},{6,2},{7,3},{8,12},{9,13},{10,... | collective-permute-start | bytes 61448 | tf_op jit(solution)/shard_map/ppermute | solution.py:52
  52.1 4.7 %collective-permute-start.12 = (f32[40,128]{1,0:T(8,128)S(1)}, f32[40,128]{1,0:T(8,128)S(1)}, u32[]{:S(2)}, u32[]{:S(2)}) collective-permute-start(f32[40,128]{1,0:T(8,128)S(1)} %get-tuple-element.47), channel_id=1, source_target_pairs={{0,6},{1,7},{2,4},{3,5},{4,2},{5,3},{6,0},{7,1},{8,14},{9,15},{10,... | collective-permute-start | bytes 61448 | tf_op jit(solution)/shard_map/ppermute | solution.py:52
